TPU v7x, 256 devices: a whole 4x4x8 slice. The times are simulated.
256 devices in a mesh: energy: 8 (over x, z_hi), strip: 32 (over y, z_lo, core).
Axes of the slice: x: 4, y: 4, z: 8 (z_hi: 2, z_lo: 4; z = z_hi * 4 + z_lo), core: 2. Of those that a mesh axis runs over, the one named last changes fastest.
Arguments:
- object_field: float32 [64, 2, 2048, 384], P('energy', None, 'strip'), may hold values from -5 to 5
- probe_modes: float32 [64, 3, 2, 128, 128], P('energy'), may hold values from -2.5 to 2.5
- measured: float32 [64, 32, 5, 128, 128], P('energy', 'strip'), may hold values from 0.5 to 3
- scan_cols: int32 [32, 5], replicated, may hold values from 0 to 256, as said below
- spectra: float32 [64, 2, 8], replicated, may hold values from -4 to 4
- material_order: int32 [8], replicated, may hold values from 0 to 7, each once
Outputs:
- refined_object: float32 [64, 2, 2048, 384], P('energy', None, 'strip')
- abundance: float32 [8, 2, 32, 64, 384], P(None, None, 'strip', 'energy')
Inputs may be any that keep to these rules, and one draw needn't show every extreme that they name: `scan_cols`: row b lists the first columns of the scan positions of band b, whose top row is b * 64; they rise, neighbours differ by 32 to 96, the first is 0 and the last 256. `material_order`: each material once.
All inputs are finite; a program needn't handle non-finite values.
Results may differ from a plain program's by a relative error of at most 0.0013.
Values sent between devices are 32-bit elements; how exact they have to be, the bound alone decides.
No kernel may reach another device: no remote copies, remote signals or barrier semaphores. Data moves between devices by JAX's collectives and lax.ppermute only.
A program may use at most 64 MiB of HBM per device.

v0:
```python
import jax
import jax.numpy as jnp
from jax import lax
from jax.sharding import PartitionSpec as P

PRECISE = lax.Precision.HIGHEST


def shifted(block, axis, distance):
    devices = range(lax.axis_size(axis))
    route = [(i - distance, i) for i in devices if i - distance in devices]
    return lax.ppermute(block, axis, route)


def dft_tables(probe_width, phase_sign):
    counter = jnp.arange(probe_width, dtype=jnp.int32)
    phase_index = counter[:, None] * counter[None, :] % probe_width
    angle_grid = phase_index.astype(jnp.float32) * (2.0 * jnp.pi / probe_width)
    root_width = jnp.sqrt(jnp.float32(probe_width))
    cosine_table = (jnp.cos(angle_grid) / root_width).astype(jnp.bfloat16)
    sine_table = (phase_sign * jnp.sin(angle_grid) / root_width).astype(jnp.bfloat16)
    blocks = jnp.stack(
        [jnp.stack([cosine_table, sine_table]), jnp.stack([-sine_table, cosine_table])]
    )
    return (blocks.transpose(0, 2, 1, 3), blocks.transpose(1, 2, 0, 3))


def transform(left_table, right_table, waves):
    first_section = jnp.einsum(
        "dacj,emcjb->emdab", left_table, waves, preferred_element_type=jnp.float32
    )
    first_section = first_section.astype(jnp.bfloat16)
    return jnp.einsum(
        "emcab,cbdk->emdak", first_section, right_table, preferred_element_type=jnp.float32
    )


def band_gradient(window, measured_band, band_cols, probe_modes, tables):
    forward_left, forward_right, inverse_left, inverse_right = tables
    probe_width = probe_modes.shape[-1]
    col_count = window.shape[-1]
    pixel_index = jnp.arange(probe_width, dtype=jnp.int32)
    col_index = jnp.arange(col_count, dtype=jnp.int32)
    placement = (
        band_cols[:, None, None] + pixel_index[None, :, None] == col_index[None, None, :]
    ).astype(jnp.float32)

    def one_energy(operands):
        window_one, measured_one, probe_one = operands
        probe_real = probe_one[None, :, 0]
        probe_imag = probe_one[None, :, 1]
        patches = jnp.einsum("crx,pjx->pcrj", window_one, placement, precision=PRECISE)
        object_real = patches[:, None, 0]
        object_imag = patches[:, None, 1]
        exit_wave = jnp.stack(
            [
                probe_real * object_real - probe_imag * object_imag,
                probe_real * object_imag + probe_imag * object_real,
            ],
            axis=2,
        ).astype(jnp.bfloat16)
        spectrum = transform(forward_left, forward_right, exit_wave)
        intensity = jnp.sum(spectrum * spectrum, axis=(1, 2))
        scaling = measured_one / jnp.sqrt(jnp.maximum(intensity, 0.25))
        corrected = (spectrum * scaling[:, None, None]).astype(jnp.bfloat16)
        returned = transform(inverse_left, inverse_right, corrected)
        residual_wave = exit_wave.astype(jnp.float32) - returned
        wave_real = residual_wave[:, :, 0]
        wave_imag = residual_wave[:, :, 1]
        grad_real = jnp.sum(probe_real * wave_real + probe_imag * wave_imag, axis=1)
        grad_imag = jnp.sum(probe_real * wave_imag - probe_imag * wave_real, axis=1)
        update = jnp.stack([grad_real, grad_imag], axis=1)
        return jnp.einsum("pcrj,pjx->crx", update, placement, precision=PRECISE)

    return lax.map(one_energy, (window, measured_band, probe_modes))


def build_basis(spectra):
    spectra_real = spectra[:, 0]
    spectra_imag = spectra[:, 1]
    upper_rows = jnp.stack([spectra_real, -spectra_imag], axis=-1)
    lower_rows = jnp.stack([spectra_imag, spectra_real], axis=-1)
    stacked = jnp.stack([upper_rows, lower_rows], axis=1)
    return stacked.reshape(2 * spectra.shape[0], 2 * spectra.shape[2])


def on_device(object_field, probe_modes, measured, scan_cols, spectra, material_order):
    probe_width = probe_modes.shape[-1]
    half_width = probe_width // 2
    forward_left, forward_right = dft_tables(probe_width, 1)
    inverse_left, inverse_right = dft_tables(probe_width, -1)
    tables = (forward_left, forward_right, inverse_left, inverse_right)
    probe_power = jnp.sum(probe_modes * probe_modes, axis=(1, 2))
    step_size = 0.5 / jnp.max(probe_power, axis=(1, 2))
    basis_matrix = build_basis(spectra)
    gram_matrix = jnp.dot(basis_matrix.T, basis_matrix, precision=PRECISE)
    factor = jnp.linalg.cholesky(gram_matrix)
    solver_map = jax.scipy.linalg.cho_solve((factor, True), basis_matrix.T)
    materials = spectra.shape[2]
    col_count = object_field.shape[3]
    strip_index = lax.axis_index("strip")
    measured_own = measured[:, 0]
    own_cols = lax.dynamic_index_in_dim(scan_cols, strip_index, 0, keepdims=False)
    estimate = object_field
    lower_rows = shifted(estimate, "strip", -1)
    window = jnp.concatenate([estimate, lower_rows], axis=2)
    gradient = band_gradient(window, measured_own, own_cols, probe_modes, tables)
    carried_rows = shifted(gradient[:, :, half_width:], "strip", 1)
    gradient_total = gradient[:, :, :half_width] + carried_rows
    estimate = estimate - step_size[:, None, None, None] * gradient_total
    gathered = lax.all_to_all(estimate, "energy", split_axis=2, concat_axis=0, tiled=True)
    sub_rows = gathered.shape[2]
    spectra_rows = gathered.reshape(2 * gathered.shape[0], sub_rows * col_count)
    coefficients = jnp.dot(solver_map, spectra_rows, precision=PRECISE)
    projected = jnp.dot(basis_matrix, coefficients, precision=PRECISE).reshape(gathered.shape)
    estimate = lax.all_to_all(projected, "energy", split_axis=0, concat_axis=2, tiled=True)
    abundance = coefficients.reshape(materials, 2, 1, sub_rows, col_count)
    abundance = jnp.take(abundance, material_order, axis=0)
    return (estimate, abundance)


def solution(mesh):
    return jax.shard_map(
        on_device,
        mesh=mesh,
        in_specs=(
            P("energy", None, "strip", None),
            P("energy", None, None, None, None),
            P("energy", "strip", None, None, None),
            P(),
            P(),
            P(),
        ),
        out_specs=(P("energy", None, "strip", None), P(None, None, "strip", "energy", None)),
        check_vma=False,
    )
```

profile of v0, /device:TPU:88, one launch (start us, length us, event | category | flops | bytes accessed | tf_op | source)
XLA Modules:
  0.0 259.8 jit_solution(14899475918422340941)
XLA Ops:
  5.0 15.8 %collective-permute-done = f32[8,2,64,384]{3,2,1,0:T(8,128)S(1)} collective-permute-done((f32[8,2,64,384]{3,2,1,0:T(8,128)}, f32[8,2,64,384]{3,2,1,0:T(8,128)S(1)}, u32[]{:S(2)}, u32[]{:S(2)}) %collective-permute-start) | collective-permute-done | bytes 1572896 | tf_op jit(solution)/shard_map/ppermute | solution.py:12
  20.8 3.3 %pad_maximum_fusion.3 = f32[8,2,128,384]{3,2,1,0:T(8,128)} fusion(f32[8,2,64,384]{3,2,1,0:T(8,128)S(1)} %collective-permute-done, f32[8,2,64,384]{3,2,1,0:T(8,128)} %param.8), kind=kLoop, calls=%fused_computation.50 | loop fusion | flops 786432 | bytes 6291456 | tf_op jit(solution)/shard_map/concatenate | solution.py:106
  24.1 115.2 %while.11 = (s32[]{:T(128)}, f32[8,2,128,384]{3,1,0,2:T(2,128)}, f32[8,3,2,128,128]{4,3,2,1,0:T(8,128)}, f32[8,2,128,384]{3,2,1,0:T(8,128)}, bf16[2,128,2,128]{3...) while((s32[]{:T(128)}, f32[8,2,128,384]{3,1,0,2:T(2,128)}, ...), condition=%wide.region_8.9_spmd.clone, body=%wide.region_4.8_spmd.clone.sunk | while | flops 2528952320 | bytes 25303212 | solution.py:75
  24.1 2.6 %convolution_bitcast_fusion.4 = f32[5,2,128,128]{3,2,0,1:T(8,128)S(1)} fusion(s32[5,128]{1,0:T(8,128)S(1)} %get-tuple-element.288, f32[8,2,128,384]{3,2,1,0:T(8,128)} %get-tuple-element.282, s32[]{:T(128)} %get-tuple-element.268), kind=kOutput, calls=%fused_computation.11.clone.1 | convolution fusion | flops 755466240 | bytes 1051648 | tf_op jit(solution)/shard_map/while/body/eval_jaxpr/crx,pjx->pcrj/dot_general | solution.py:52
  32.6 2.6 bitcast_subtract_fusion.2
  38.6 2.6 %convolution_bitcast_fusion.4 = f32[5,2,128,128]{3,2,0,1:T(8,128)S(1)} fusion(s32[5,128]{1,0:T(8,128)S(1)} %get-tuple-element.288, f32[8,2,128,384]{3,2,1,0:T(8,128)} %get-tuple-element.282, s32[]{:T(128)} %get-tuple-element.268), kind=kOutput, calls=%fused_computation.11.clone.1 | convolution fusion | flops 755466240 | bytes 1051648 | tf_op jit(solution)/shard_map/while/body/eval_jaxpr/crx,pjx->pcrj/dot_general | solution.py:52
  47.0 2.6 bitcast_subtract_fusion.2
  52.9 2.6 %convolution_bitcast_fusion.4 = f32[5,2,128,128]{3,2,0,1:T(8,128)S(1)} fusion(s32[5,128]{1,0:T(8,128)S(1)} %get-tuple-element.288, f32[8,2,128,384]{3,2,1,0:T(8,128)} %get-tuple-element.282, s32[]{:T(128)} %get-tuple-element.268), kind=kOutput, calls=%fused_computation.11.clone.1 | convolution fusion | flops 755466240 | bytes 1051648 | tf_op jit(solution)/shard_map/while/body/eval_jaxpr/crx,pjx->pcrj/dot_general | solution.py:52
  67.3 2.6 %convolution_bitcast_fusion.4 = f32[5,2,128,128]{3,2,0,1:T(8,128)S(1)} fusion(s32[5,128]{1,0:T(8,128)S(1)} %get-tuple-element.288, f32[8,2,128,384]{3,2,1,0:T(8,128)} %get-tuple-element.282, s32[]{:T(128)} %get-tuple-element.268), kind=kOutput, calls=%fused_computation.11.clone.1 | convolution fusion | flops 755466240 | bytes 1051648 | tf_op jit(solution)/shard_map/while/body/eval_jaxpr/crx,pjx->pcrj/dot_general | solution.py:52
  75.8 2.6 bitcast_subtract_fusion.2
  81.7 2.6 %convolution_bitcast_fusion.4 = f32[5,2,128,128]{3,2,0,1:T(8,128)S(1)} fusion(s32[5,128]{1,0:T(8,128)S(1)} %get-tuple-element.288, f32[8,2,128,384]{3,2,1,0:T(8,128)} %get-tuple-element.282, s32[]{:T(128)} %get-tuple-element.268), kind=kOutput, calls=%fused_computation.11.clone.1 | convolution fusion | flops 755466240 | bytes 1051648 | tf_op jit(solution)/shard_map/while/body/eval_jaxpr/crx,pjx->pcrj/dot_general | solution.py:52
  96.2 2.6 %convolution_bitcast_fusion.4 = f32[5,2,128,128]{3,2,0,1:T(8,128)S(1)} fusion(s32[5,128]{1,0:T(8,128)S(1)} %get-tuple-element.288, f32[8,2,128,384]{3,2,1,0:T(8,128)} %get-tuple-element.282, s32[]{:T(128)} %get-tuple-element.268), kind=kOutput, calls=%fused_computation.11.clone.1 | convolution fusion | flops 755466240 | bytes 1051648 | tf_op jit(solution)/shard_map/while/body/eval_jaxpr/crx,pjx->pcrj/dot_general | solution.py:52
  104.6 2.6 bitcast_subtract_fusion.2
  110.5 2.6 %convolution_bitcast_fusion.4 = f32[5,2,128,128]{3,2,0,1:T(8,128)S(1)} fusion(s32[5,128]{1,0:T(8,128)S(1)} %get-tuple-element.288, f32[8,2,128,384]{3,2,1,0:T(8,128)} %get-tuple-element.282, s32[]{:T(128)} %get-tuple-element.268), kind=kOutput, calls=%fused_computation.11.clone.1 | convolution fusion | flops 755466240 | bytes 1051648 | tf_op jit(solution)/shard_map/while/body/eval_jaxpr/crx,pjx->pcrj/dot_general | solution.py:52
  124.9 2.6 %convolution_bitcast_fusion.4 = f32[5,2,128,128]{3,2,0,1:T(8,128)S(1)} fusion(s32[5,128]{1,0:T(8,128)S(1)} %get-tuple-element.288, f32[8,2,128,384]{3,2,1,0:T(8,128)} %get-tuple-element.282, s32[]{:T(128)} %get-tuple-element.268), kind=kOutput, calls=%fused_computation.11.clone.1 | convolution fusion | flops 755466240 | bytes 1051648 | tf_op jit(solution)/shard_map/while/body/eval_jaxpr/crx,pjx->pcrj/dot_general | solution.py:52
  133.4 2.6 bitcast_subtract_fusion.2
  139.3 3.2 %slice.51 = f32[8,2,64,384]{3,1,0,2:T(2,128)} slice(f32[8,2,128,384]{3,1,0,2:T(2,128)} %get-tuple-element.54), slice={[0:8], [0:2], [64:128], [0:384]} | slice | bytes 3145728 | tf_op jit(solution)/shard_map/slice | solution.py:108
  142.6 4.1 %collective-permute-start.1 = (f32[8,2,64,384]{3,1,0,2:T(2,128)}, f32[8,2,64,384]{3,1,0,2:T(2,128)}, u32[]{:S(2)}, u32[]{:S(2)}) collective-permute-start(f32[8,2,64,384]{3,1,0,2:T(2,128)} %slice.51), channel_id=1, source_target_pairs={{0,1},{1,2},{2,3},{3,4},{4,5},{5,6},{6,7},{7,8},{8,9},{9,10},{10,1... | collective-permute-start | bytes 4718600 | tf_op jit(solution)/shard_map/ppermute | solution.py:12
  147.2 17.6 %collective-permute-done.1 = f32[8,2,64,384]{3,1,0,2:T(2,128)} collective-permute-done((f32[8,2,64,384]{3,1,0,2:T(2,128)}, f32[8,2,64,384]{3,1,0,2:T(2,128)}, u32[]{:S(2)}, u32[]{:S(2)}) %collective-permute-start.1) | collective-permute-done | bytes 1572896 | tf_op jit(solution)/shard_map/ppermute | solution.py:12
  164.8 5.0 %copy_subtract_fusion = f32[8,2,64,384]{3,1,0,2:T(2,128)} fusion(f32[8,2,64,384]{3,2,1,0:T(8,128)S(1)} %copy-done.2, f32[8,2,64,384]{3,1,0,2:T(2,128)} %collective-permute-done.1, f32[8,2,128,384]{3,1,0,2:T(2,128)} %get-tuple-element.54, f32[8]{0:T(128)S(1)} %broadcast_divide_fusion), kind=kLoop, calls=%fused_computation.53 | loop fusion | flops 1179648 | bytes 6291488 | tf_op jit(solution)/shard_map/sub | solution.py:110
  169.8 9.7 %all-to-all-start = ((f32[8,2,64,384]{3,1,0,2:T(2,128)}), f32[8,2,64,384]{3,1,0,2:T(2,128)S(1)}, u32[]{:S(2)}, u32[]{:S(2)}) async-start(f32[8,2,64,384]{3,1,0,2:T(2,128)} %copy_subtract_fusion), calls=%async_computation | async-start | bytes 3145728 | tf_op jit(solution)/shard_map/all_to_all | solution.py:111
  184.6 35.8 %all-to-all-done = f32[8,2,64,384]{3,1,0,2:T(2,128)S(1)} async-done(((f32[8,2,64,384]{3,1,0,2:T(2,128)}), f32[8,2,64,384]{3,1,0,2:T(2,128)S(1)}, u32[]{:S(2)}, u32[]{:S(2)}) %all-to-all-start) | async-done | bytes 1572896 | tf_op jit(solution)/shard_map/all_to_all | solution.py:111
  225.6 11.2 %all-to-all-start.1 = ((f32[64,2,8,384]{3,2,1,0:T(8,128)}), f32[64,2,8,384]{3,2,1,0:T(8,128)S(1)}, u32[]{:S(2)}, u32[]{:S(2)}) async-start(f32[64,2,8,384]{3,2,1,0:T(8,128)} %copy.87), calls=%async_computation.1 | async-start | bytes 3145728 | tf_op jit(solution)/shard_map/all_to_all | solution.py:116
  238.2 20.3 %all-to-all-done.1 = f32[64,2,8,384]{3,2,1,0:T(8,128)S(1)} async-done(((f32[64,2,8,384]{3,2,1,0:T(8,128)}), f32[64,2,8,384]{3,2,1,0:T(8,128)S(1)}, u32[]{:S(2)}, u32[]{:S(2)}) %all-to-all-start.1) | async-done | bytes 1572896 | tf_op jit(solution)/shard_map/all_to_all | solution.py:116
  (201 shorter events, 98.4 us)
Async XLA Ops:
  0.6 20.2 %collective-permute-start = (f32[8,2,64,384]{3,2,1,0:T(8,128)}, f32[8,2,64,384]{3,2,1,0:T(8,128)S(1)}, u32[]{:S(2)}, u32[]{:S(2)}) collective-permute-start(f32[8,2,64,384]{3,2,1,0:T(8,128)} %param.8), channel_id=1, source_target_pairs={{1,0},{2,1},{3,2},{4,3},{5,4},{6,5},{7,6},{8,7},{9,8},{10,9},{11,1... | collective-permute-start | bytes 4718600 | tf_op jit(solution)/shard_map/ppermute | solution.py:12
  24.1 4.5 %copy-start.3 = (bf16[2,128,2,128]{3,1,0,2:T(8,128)(2,1)}, bf16[2,128,2,128]{3,1,0,2:T(8,128)(2,1)S(1)}, u32[]{:S(2)}) copy-start(bf16[2,128,2,128]{3,1,0,2:T(8,128)(2,1)S(1)} %get-tuple-element.284) | copy-start | bytes 393220 | tf_op jit(solution)/shard_map/while
  35.5 3.0 %copy-start.4 = (bf16[2,128,2,128]{3,1,0,2:T(8,128)(2,1)S(1)}, bf16[2,128,2,128]{3,1,0,2:T(8,128)(2,1)}, u32[]{:S(2)}) copy-start(bf16[2,128,2,128]{3,1,0,2:T(8,128)(2,1)} %copy-done.3) | copy-start | bytes 393220 | tf_op jit(solution)/shard_map/while
  38.6 4.5 %copy-start.3 = (bf16[2,128,2,128]{3,1,0,2:T(8,128)(2,1)}, bf16[2,128,2,128]{3,1,0,2:T(8,128)(2,1)S(1)}, u32[]{:S(2)}) copy-start(bf16[2,128,2,128]{3,1,0,2:T(8,128)(2,1)S(1)} %get-tuple-element.284) | copy-start | bytes 393220 | tf_op jit(solution)/shard_map/while
  49.9 3.0 %copy-start.4 = (bf16[2,128,2,128]{3,1,0,2:T(8,128)(2,1)S(1)}, bf16[2,128,2,128]{3,1,0,2:T(8,128)(2,1)}, u32[]{:S(2)}) copy-start(bf16[2,128,2,128]{3,1,0,2:T(8,128)(2,1)} %copy-done.3) | copy-start | bytes 393220 | tf_op jit(solution)/shard_map/while
  52.9 4.5 %copy-start.3 = (bf16[2,128,2,128]{3,1,0,2:T(8,128)(2,1)}, bf16[2,128,2,128]{3,1,0,2:T(8,128)(2,1)S(1)}, u32[]{:S(2)}) copy-start(bf16[2,128,2,128]{3,1,0,2:T(8,128)(2,1)S(1)} %get-tuple-element.284) | copy-start | bytes 393220 | tf_op jit(solution)/shard_map/while
  64.3 3.0 %copy-start.4 = (bf16[2,128,2,128]{3,1,0,2:T(8,128)(2,1)S(1)}, bf16[2,128,2,128]{3,1,0,2:T(8,128)(2,1)}, u32[]{:S(2)}) copy-start(bf16[2,128,2,128]{3,1,0,2:T(8,128)(2,1)} %copy-done.3) | copy-start | bytes 393220 | tf_op jit(solution)/shard_map/while
  67.3 4.5 %copy-start.3 = (bf16[2,128,2,128]{3,1,0,2:T(8,128)(2,1)}, bf16[2,128,2,128]{3,1,0,2:T(8,128)(2,1)S(1)}, u32[]{:S(2)}) copy-start(bf16[2,128,2,128]{3,1,0,2:T(8,128)(2,1)S(1)} %get-tuple-element.284) | copy-start | bytes 393220 | tf_op jit(solution)/shard_map/while
  78.7 3.0 %copy-start.4 = (bf16[2,128,2,128]{3,1,0,2:T(8,128)(2,1)S(1)}, bf16[2,128,2,128]{3,1,0,2:T(8,128)(2,1)}, u32[]{:S(2)}) copy-start(bf16[2,128,2,128]{3,1,0,2:T(8,128)(2,1)} %copy-done.3) | copy-start | bytes 393220 | tf_op jit(solution)/shard_map/while
  81.7 4.5 %copy-start.3 = (bf16[2,128,2,128]{3,1,0,2:T(8,128)(2,1)}, bf16[2,128,2,128]{3,1,0,2:T(8,128)(2,1)S(1)}, u32[]{:S(2)}) copy-start(bf16[2,128,2,128]{3,1,0,2:T(8,128)(2,1)S(1)} %get-tuple-element.284) | copy-start | bytes 393220 | tf_op jit(solution)/shard_map/while
  93.1 3.0 %copy-start.4 = (bf16[2,128,2,128]{3,1,0,2:T(8,128)(2,1)S(1)}, bf16[2,128,2,128]{3,1,0,2:T(8,128)(2,1)}, u32[]{:S(2)}) copy-start(bf16[2,128,2,128]{3,1,0,2:T(8,128)(2,1)} %copy-done.3) | copy-start | bytes 393220 | tf_op jit(solution)/shard_map/while
  96.2 4.5 %copy-start.3 = (bf16[2,128,2,128]{3,1,0,2:T(8,128)(2,1)}, bf16[2,128,2,128]{3,1,0,2:T(8,128)(2,1)S(1)}, u32[]{:S(2)}) copy-start(bf16[2,128,2,128]{3,1,0,2:T(8,128)(2,1)S(1)} %get-tuple-element.284) | copy-start | bytes 393220 | tf_op jit(solution)/shard_map/while
  107.5 3.0 %copy-start.4 = (bf16[2,128,2,128]{3,1,0,2:T(8,128)(2,1)S(1)}, bf16[2,128,2,128]{3,1,0,2:T(8,128)(2,1)}, u32[]{:S(2)}) copy-start(bf16[2,128,2,128]{3,1,0,2:T(8,128)(2,1)} %copy-done.3) | copy-start | bytes 393220 | tf_op jit(solution)/shard_map/while
  110.5 4.5 %copy-start.3 = (bf16[2,128,2,128]{3,1,0,2:T(8,128)(2,1)}, bf16[2,128,2,128]{3,1,0,2:T(8,128)(2,1)S(1)}, u32[]{:S(2)}) copy-start(bf16[2,128,2,128]{3,1,0,2:T(8,128)(2,1)S(1)} %get-tuple-element.284) | copy-start | bytes 393220 | tf_op jit(solution)/shard_map/while
  121.9 3.0 %copy-start.4 = (bf16[2,128,2,128]{3,1,0,2:T(8,128)(2,1)S(1)}, bf16[2,128,2,128]{3,1,0,2:T(8,128)(2,1)}, u32[]{:S(2)}) copy-start(bf16[2,128,2,128]{3,1,0,2:T(8,128)(2,1)} %copy-done.3) | copy-start | bytes 393220 | tf_op jit(solution)/shard_map/while
  124.9 4.5 %copy-start.3 = (bf16[2,128,2,128]{3,1,0,2:T(8,128)(2,1)}, bf16[2,128,2,128]{3,1,0,2:T(8,128)(2,1)S(1)}, u32[]{:S(2)}) copy-start(bf16[2,128,2,128]{3,1,0,2:T(8,128)(2,1)S(1)} %get-tuple-element.284) | copy-start | bytes 393220 | tf_op jit(solution)/shard_map/while
  136.3 3.0 %copy-start.4 = (bf16[2,128,2,128]{3,1,0,2:T(8,128)(2,1)S(1)}, bf16[2,128,2,128]{3,1,0,2:T(8,128)(2,1)}, u32[]{:S(2)}) copy-start(bf16[2,128,2,128]{3,1,0,2:T(8,128)(2,1)} %copy-done.3) | copy-start | bytes 393220 | tf_op jit(solution)/shard_map/while
  139.3 7.4 %copy-start.1 = (f32[8,3,2,128,128]{4,3,2,1,0:T(8,128)S(1)}, f32[8,3,2,128,128]{4,3,2,1,0:T(8,128)}, u32[]{:S(2)}) copy-start(f32[8,3,2,128,128]{4,3,2,1,0:T(8,128)} %get-tuple-element.290) | copy-start | bytes 9437188
  142.6 22.2 %copy-start.2 = (f32[8,2,64,384]{3,2,1,0:T(8,128)S(1)}, f32[8,2,64,384]{3,2,1,0:T(8,128)}, u32[]{:S(2)}) copy-start(f32[8,2,64,384]{3,2,1,0:T(8,128)} %param.8) | copy-start | bytes 4718596
  142.6 22.2 %collective-permute-start.1 = (f32[8,2,64,384]{3,1,0,2:T(2,128)}, f32[8,2,64,384]{3,1,0,2:T(2,128)}, u32[]{:S(2)}, u32[]{:S(2)}) collective-permute-start(f32[8,2,64,384]{3,1,0,2:T(2,128)} %slice.51), channel_id=1, source_target_pairs={{0,1},{1,2},{2,3},{3,4},{4,5},{5,6},{6,7},{7,8},{8,9},{9,10},{10,1... | collective-permute-start | bytes 4718600 | tf_op jit(solution)/shard_map/ppermute | solution.py:12
  169.8 9.7 %copy-start.5 = (f32[64,2,8]{0,2,1:T(8,128)S(1)}, f32[64,2,8]{0,2,1:T(8,128)}, u32[]{:S(2)}) copy-start(f32[64,2,8]{0,2,1:T(8,128)} %param.12) | copy-start | bytes 12292
  169.8 50.7 %all-to-all-start = ((f32[8,2,64,384]{3,1,0,2:T(2,128)}), f32[8,2,64,384]{3,1,0,2:T(2,128)S(1)}, u32[]{:S(2)}, u32[]{:S(2)}) async-start(f32[8,2,64,384]{3,1,0,2:T(2,128)} %copy_subtract_fusion), calls=%async_computation | async-start | bytes 3145728 | tf_op jit(solution)/shard_map/all_to_all | solution.py:111
  225.6 11.3 %copy-start.6 = (s32[8]{0:T(128)S(1)}, s32[8]{0:T(128)}, u32[]{:S(2)}) copy-start(s32[8]{0:T(128)} %param.13) | copy-start | bytes 100
  225.6 33.0 %all-to-all-start.1 = ((f32[64,2,8,384]{3,2,1,0:T(8,128)}), f32[64,2,8,384]{3,2,1,0:T(8,128)S(1)}, u32[]{:S(2)}, u32[]{:S(2)}) async-start(f32[64,2,8,384]{3,2,1,0:T(8,128)} %copy.87), calls=%async_computation.1 | async-start | bytes 3145728 | tf_op jit(solution)/shard_map/all_to_all | solution.py:116
  (1 other events, 2.0 us)
where the time goes:
time: 261 us; the launch traced here: 260 us
  waiting for transfers between devices  89.5 us (34%)
  matrix products  74.2 us (28%)
  other arithmetic  34.5 us (13%)
  local copies, waits for them, and re-layouts  33.2 us (13%)
  starting transfers between devices  27 us (10%)
    dot_general x16, matrix products, transform(): jnp.einsum('emcab,cbdk->emdak', first_section, right_table, preferred_ele...  38.3 us
    all_to_all x1, waiting for transfers between devices, on_device(): lax.all_to_all(estimate, 'energy', split_axis=2, concat_axis=0, tiled=True)  35.8 us
    ppermute x2, waiting for transfers between devices, shifted(): return lax.ppermute(block, axis, route)  33.4 us
    dot_general x8, matrix products, one_energy(): jnp.einsum('crx,pjx->pcrj', window_one, placement, precision=PRECISE)  20.8 us
    all_to_all x1, waiting for transfers between devices, on_device(): lax.all_to_all(projected, 'energy', split_axis=0, concat_axis=2, tiled=True)  20.3 us
    div x8, other arithmetic, one_energy(): scaling = measured_one / jnp.sqrt(jnp.maximum(intensity, 0.25))  14.1 us
    dot_general x8, matrix products, one_energy(): return jnp.einsum('pcrj,pjx->crx', update, placement, precision=PRECISE)  12.3 us
    all_to_all x1, starting transfers between devices, on_device(): lax.all_to_all(projected, 'energy', split_axis=0, concat_axis=2, tiled=True)  11.2 us
  transfers between devices with their start and end apart: 4, of which 4 were waited for; matrix products, arithmetic and copies ran while one was open for 4% of the time, Pallas kernels for 0%

commit v1 on v0

v1 whole, which is shorter than its diff:
```python
import functools

import jax
import jax.numpy as jnp
import numpy as np
from jax import lax
from jax.experimental import pallas as pl
from jax.experimental.pallas import tpu as pltpu
from jax.sharding import PartitionSpec as P

PRECISE = lax.Precision.HIGHEST
LANES = 128


def shifted(block, axis, distance):
    devices = range(lax.axis_size(axis))
    route = [(i - distance, i) for i in devices if i - distance in devices]
    return lax.ppermute(block, axis, route)


def dft_tables(width):
    counter = np.arange(width)
    angle = 2.0 * np.pi * (counter[:, None] * counter[None, :] % width) / width
    cosine = (np.cos(angle) / np.sqrt(width)).astype(np.float32)
    sine = (np.sin(angle) / np.sqrt(width)).astype(np.float32)
    left = np.block([[cosine, sine], [-sine, cosine]])
    right = np.block([[cosine, -sine], [sine, cosine]])
    return jnp.asarray(left).astype(jnp.bfloat16), jnp.asarray(right).astype(jnp.bfloat16)


def transform(left, right, waves):
    width = waves[0][0].shape[0]
    stacked = jnp.concatenate([jnp.concatenate(pair, axis=0) for pair in waves], axis=1)
    half = jnp.dot(left, stacked, preferred_element_type=jnp.float32).astype(jnp.bfloat16)
    rows = []
    for m in range(len(waves)):
        cols = slice(m * width, (m + 1) * width)
        rows.append(jnp.concatenate([half[:width, cols], half[width:, cols]], axis=1))
    full = jnp.dot(
        jnp.concatenate(rows, axis=0), right, preferred_element_type=jnp.float32
    )
    return [
        (full[m * width:(m + 1) * width, :width], full[m * width:(m + 1) * width, width:])
        for m in range(len(waves))
    ]


def gradient_kernel(
    cols_ref, left_ref, right_ref, top_ref, low_ref, probe_ref, measured_ref,
    own_ref, carried_ref, total,
):
    modes = probe_ref.shape[1]
    width = probe_ref.shape[-1]
    half = width // 2
    positions = measured_ref.shape[1]
    blocks = total.shape[-1] // LANES
    left = left_ref[...]
    right = right_ref[...]
    lane = lax.broadcasted_iota(jnp.int32, (width, width), 1)
    power = jnp.zeros((width, width), jnp.float32)
    for m in range(modes):
        power += probe_ref[0, m, 0] * probe_ref[0, m, 0] + probe_ref[0, m, 1] * probe_ref[0, m, 1]
    peak = jnp.max(jnp.max(power, axis=0, keepdims=True), axis=1, keepdims=True)
    step = 0.5 / peak
    total[...] = jnp.zeros_like(total)

    def window(part, start):
        cols = pl.ds(pl.multiple_of(start, LANES), LANES)
        return jnp.concatenate([top_ref[0, part, :, cols], low_ref[0, part, :, cols]], axis=0)

    for p in range(positions):
        column = cols_ref[p]
        first = column // LANES * LANES
        second = jnp.minimum(first + LANES, (blocks - 1) * LANES)
        offset = column - first
        back = lax.rem(LANES - offset, LANES)
        patch = []
        for part in range(2):
            here = pltpu.roll(window(part, first), back, 1)
            there = pltpu.roll(window(part, second), back, 1)
            patch.append(jnp.where(lane < LANES - offset, here, there))
        waves = []
        for m in range(modes):
            pr, pi = probe_ref[0, m, 0], probe_ref[0, m, 1]
            waves.append((
                (pr * patch[0] - pi * patch[1]).astype(jnp.bfloat16),
                (pr * patch[1] + pi * patch[0]).astype(jnp.bfloat16),
            ))
        spectrum = transform(left, right, waves)
        intensity = sum(r * r + i * i for r, i in spectrum)
        scale = measured_ref[0, p] * lax.rsqrt(jnp.maximum(intensity, 0.25))
        flipped = -scale
        corrected = [
            ((r * scale).astype(jnp.bfloat16), (i * flipped).astype(jnp.bfloat16))
            for r, i in spectrum
        ]
        returned = transform(left, right, corrected)
        grad_real = grad_imag = None
        for m in range(modes):
            pr, pi = probe_ref[0, m, 0], probe_ref[0, m, 1]
            wr = waves[m][0].astype(jnp.float32) - returned[m][0]
            wi = waves[m][1].astype(jnp.float32) + returned[m][1]
            gr = pr * wr + pi * wi
            gi = pr * wi - pi * wr
            grad_real = gr if m == 0 else grad_real + gr
            grad_imag = gi if m == 0 else grad_imag + gi
        for part, grad in enumerate((grad_real, grad_imag)):
            moved = pltpu.roll(grad, offset, 1)
            here = pl.ds(pl.multiple_of(first, LANES), LANES)
            there = pl.ds(pl.multiple_of(second, LANES), LANES)
            total[part, :, here] += jnp.where(lane >= offset, moved, 0.0)
            total[part, :, there] += jnp.where(lane < offset, moved, 0.0)
    own_ref[0] = top_ref[0] - step * total[:, :half]
    carried_ref[0] = step * total[:, half:]


def band_update(own_cols, left, right, top, low, probe, measured):
    energies, parts, rows, cols = top.shape
    _, modes, _, width, _ = probe.shape
    positions = measured.shape[1]
    band = pl.BlockSpec((1, parts, rows, cols), lambda e: (e, 0, 0, 0))
    table = pl.BlockSpec(left.shape, lambda e: (0, 0))
    return pl.pallas_call(
        gradient_kernel,
        grid=(energies,),
        in_specs=[
            pl.BlockSpec(memory_space=pltpu.SMEM),
            table,
            table,
            band,
            band,
            pl.BlockSpec((1, modes, parts, width, width), lambda e: (e, 0, 0, 0, 0)),
            pl.BlockSpec((1, positions, width, width), lambda e: (e, 0, 0, 0)),
        ],
        out_specs=[band, band],
        out_shape=[jax.ShapeDtypeStruct(top.shape, jnp.float32)] * 2,
        scratch_shapes=[pltpu.VMEM((parts, width, cols), jnp.float32)],
        name="band_update",
    )(own_cols, left, right, top, low, probe, measured)


def build_basis(spectra):
    spectra_real = spectra[:, 0]
    spectra_imag = spectra[:, 1]
    upper_rows = jnp.stack([spectra_real, -spectra_imag], axis=-1)
    lower_rows = jnp.stack([spectra_imag, spectra_real], axis=-1)
    stacked = jnp.stack([upper_rows, lower_rows], axis=1)
    return stacked.reshape(2 * spectra.shape[0], 2 * spectra.shape[2])


def on_device(object_field, probe_modes, measured, scan_cols, spectra, material_order):
    left, right = dft_tables(probe_modes.shape[-1])
    basis_matrix = build_basis(spectra)
    gram_matrix = jnp.dot(basis_matrix.T, basis_matrix, precision=PRECISE)
    factor = jnp.linalg.cholesky(gram_matrix)
    solver_map = jax.scipy.linalg.cho_solve((factor, True), basis_matrix.T)
    materials = spectra.shape[2]
    col_count = object_field.shape[3]
    strip_index = lax.axis_index("strip")
    own_cols = lax.dynamic_index_in_dim(scan_cols, strip_index, 0, keepdims=False)
    lower_rows = shifted(object_field, "strip", -1)
    own, carried = band_update(
        own_cols, left, right, object_field, lower_rows, probe_modes, measured[:, 0]
    )
    estimate = own - shifted(carried, "strip", 1)
    gathered = lax.all_to_all(estimate, "energy", split_axis=2, concat_axis=0, tiled=True)
    sub_rows = gathered.shape[2]
    spectra_rows = gathered.reshape(2 * gathered.shape[0], sub_rows * col_count)
    coefficients = jnp.dot(solver_map, spectra_rows, precision=PRECISE)
    projected = jnp.dot(basis_matrix, coefficients, precision=PRECISE).reshape(gathered.shape)
    estimate = lax.all_to_all(projected, "energy", split_axis=0, concat_axis=2, tiled=True)
    abundance = coefficients.reshape(materials, 2, 1, sub_rows, col_count)
    abundance = jnp.take(abundance, material_order, axis=0)
    return (estimate, abundance)


def solution(mesh):
    return jax.shard_map(
        on_device,
        mesh=mesh,
        in_specs=(
            P("energy", None, "strip", None),
            P("energy", None, None, None, None),
            P("energy", "strip", None, None, None),
            P(),
            P(),
            P(),
        ),
        out_specs=(P("energy", None, "strip", None), P(None, None, "strip", "energy", None)),
        check_vma=False,
    )
```

time: 261 us -> 169 us (0.65)
  matrix products: 74.2 us -> 2.73 us
  Pallas kernels: 0 us -> 30.8 us
  other arithmetic: 34.5 us -> 6.47 us
  local copies, waits for them, and re-layouts: 33.2 us -> 9.53 us
    dot_general x32 -> x0, matrix products: 71.5 us -> none  [the longest x16 38.3 us: transform(): jnp.einsum('emcab,cbdk->emdak', first_section, right_table, preferred_ele...]
    pallas_call x0 -> x1, Pallas kernels: none -> 30.8 us  [band_update(): pl.pallas_call(gradient_kernel, grid=(energies,), in_specs=[pl.BlockSpec(...]
    div x9 -> x0, other arithmetic: 14.1 us -> none  [the longest x8 14.1 us: one_energy(): scaling = measured_one / jnp.sqrt(jnp.maximum(intensity, 0.25))]
    dynamic_slice x16 -> x0, local copies, waits for them, and re-layouts: 9.52 us -> none  [band_gradient(): return lax.map(one_energy, (window, measured_band, probe_modes))]
    dynamic_update_slice x8 -> x0, local copies, waits for them, and re-layouts: 8.94 us -> none  [band_gradient(): return lax.map(one_energy, (window, measured_band, probe_modes))]
    concatenate x1 -> x0, other arithmetic: 3.34 us -> none  [on_device(): window = jnp.concatenate([estimate, lower_rows], axis=2)]
    sub x1, other arithmetic: 4.98 us -> 1.64 us  [on_device(): estimate = own - shifted(carried, 'strip', 1)]
    slice x1 -> x0, local copies, waits for them, and re-layouts: 3.24 us -> none  [on_device(): carried_rows = shifted(gradient[:, :, half_width:], 'strip', 1)]
where the time goes in v1:
time: 169 us; the launch traced here: 168 us
  waiting for transfers between devices  90.8 us (54%)
  Pallas kernels  30.8 us (18%)
  starting transfers between devices  26.8 us (16%)
  local copies, waits for them, and re-layouts  9.53 us (6%)
  other arithmetic  6.47 us (4%)
  matrix products  2.73 us (2%)
    all_to_all x1, waiting for transfers between devices, on_device(): lax.all_to_all(estimate, 'energy', split_axis=2, concat_axis=0, tiled=True)  35.9 us
    ppermute x2, waiting for transfers between devices, shifted(): return lax.ppermute(block, axis, route)  35.5 us
    pallas_call x1, Pallas kernels, band_update(): pl.pallas_call(gradient_kernel, grid=(energies,), in_specs=[pl.BlockSpec(...  30.8 us
    all_to_all x1, waiting for transfers between devices, on_device(): lax.all_to_all(projected, 'energy', split_axis=0, concat_axis=2, tiled=True)  19.3 us
    all_to_all x1, starting transfers between devices, on_device(): lax.all_to_all(projected, 'energy', split_axis=0, concat_axis=2, tiled=True)  11.3 us
    all_to_all x1, starting transfers between devices, on_device(): lax.all_to_all(estimate, 'energy', split_axis=2, concat_axis=0, tiled=True)  9.69 us
    ppermute x2, starting transfers between devices, shifted(): return lax.ppermute(block, axis, route)  5.87 us
  transfers between devices with their start and end apart: 4, of which 4 were waited for; matrix products, arithmetic and copies ran while one was open for 4% of the time, Pallas kernels for 0%

profile of v1, /device:TPU:88, one launch (start us, length us, event | category | flops | bytes accessed | tf_op | source)
XLA Modules:
  0.0 167.9 jit_solution(10938144062181921151)
XLA Ops:
  0.6 1.9 %collective-permute-start = (f32[8,2,64,384]{3,2,1,0:T(8,128)}, f32[8,2,64,384]{3,2,1,0:T(8,128)S(1)}, u32[]{:S(2)}, u32[]{:S(2)}) collective-permute-start(f32[8,2,64,384]{3,2,1,0:T(8,128)} %top_ref.1), channel_id=1, source_target_pairs={{1,0},{2,1},{3,2},{4,3},{5,4},{6,5},{7,6},{8,7},{9,8},{10,9},{11,1... | collective-permute-start | bytes 4718600 | tf_op jit(solution)/shard_map/ppermute | solution.py:18
  2.6 0.7 dynamic-slice_reduce_fusion.cols_ref
  3.3 17.5 %collective-permute-done.low_ref = f32[8,2,64,384]{3,2,1,0:T(8,128)S(1)} collective-permute-done((f32[8,2,64,384]{3,2,1,0:T(8,128)}, f32[8,2,64,384]{3,2,1,0:T(8,128)S(1)}, u32[]{:S(2)}, u32[]{:S(2)}) %collective-permute-start) | collective-permute-done | bytes 1572896 | tf_op jit(solution)/shard_map/ppermute | solution.py:18
  20.8 1.1 copy-done.1
  21.9 30.8 %band_update.1 = (f32[8,2,64,384]{3,2,1,0:T(8,128)}, f32[8,2,64,384]{3,2,1,0:T(8,128)}) custom-call(s32[5]{0:T(128)} %dynamic-slice_reduce_fusion.cols_ref, bf16[256,256]{1,0:T(8,128)(2,1)} %constant.80.left_ref, bf16[256,256]{1,0:T(8,128)(2,1)} %constant.81.right_ref, f32[8,2,64,384]{3,2,1,0:T(8,128)} %top_ref.1, f32[8,2,64,384]{3,2,1,0:T(8,128)} %copy-done.1, ...), custom_call_target="tpu_custom_call" | custom-call | tf_op jit(solution)/shard_map/band_update/pallas_call | solution.py:123
  52.8 4.0 %collective-permute-start.1 = (f32[8,2,64,384]{3,2,1,0:T(8,128)}, f32[8,2,64,384]{3,2,1,0:T(8,128)S(1)}, u32[]{:S(2)}, u32[]{:S(2)}) collective-permute-start(f32[8,2,64,384]{3,2,1,0:T(8,128)} %get-tuple-element.5), channel_id=1, source_target_pairs={{0,1},{1,2},{2,3},{3,4},{4,5},{5,6},{6,7},{7,8},{8,9},{9,10},{10,1... | collective-permute-start | bytes 4718600 | tf_op jit(solution)/shard_map/ppermute | solution.py:18
  56.7 18.0 %collective-permute-done.1 = f32[8,2,64,384]{3,2,1,0:T(8,128)S(1)} collective-permute-done((f32[8,2,64,384]{3,2,1,0:T(8,128)}, f32[8,2,64,384]{3,2,1,0:T(8,128)S(1)}, u32[]{:S(2)}, u32[]{:S(2)}) %collective-permute-start.1) | collective-permute-done | bytes 1572896 | tf_op jit(solution)/shard_map/ppermute | solution.py:18
  74.7 1.6 sub.3
  76.4 2.4 %copy.26 = f32[8,2,64,384]{3,1,0,2:T(2,128)} copy(f32[8,2,64,384]{3,2,1,0:T(8,128)S(1)} %sub.3) | data formatting | bytes 3145728 | tf_op jit(solution)/shard_map/sub | solution.py:165
  78.7 9.7 %all-to-all-start = ((f32[8,2,64,384]{3,1,0,2:T(2,128)}), f32[8,2,64,384]{3,1,0,2:T(2,128)S(1)}, u32[]{:S(2)}, u32[]{:S(2)}) async-start(f32[8,2,64,384]{3,1,0,2:T(2,128)} %copy.26), calls=%async_computation | async-start | bytes 3145728 | tf_op jit(solution)/shard_map/all_to_all | solution.py:166
  89.2 1.5 cholesky.16
  90.7 0.6 compare_reduce_fusion
  91.4 0.6 fusion.4
  92.0 1.2 custom-call.10
  93.6 35.9 %all-to-all-done = f32[8,2,64,384]{3,1,0,2:T(2,128)S(1)} async-done(((f32[8,2,64,384]{3,1,0,2:T(2,128)}), f32[8,2,64,384]{3,1,0,2:T(2,128)S(1)}, u32[]{:S(2)}, u32[]{:S(2)}) %all-to-all-start) | async-done | bytes 1572896 | tf_op jit(solution)/shard_map/all_to_all | solution.py:166
  129.5 0.5 copy.27
  130.3 0.8 fusion.15
  131.1 1.4 fusion
  132.6 2.1 %copy.29 = f32[64,2,8,384]{3,2,1,0:T(8,128)} copy(f32[64,2,8,384]{3,0,2,1:T(8,128)S(1)} %fusion) | data formatting | bytes 3145728 | tf_op jit(solution)/shard_map/dot_general | solution.py:170
  134.6 11.3 %all-to-all-start.1 = ((f32[64,2,8,384]{3,2,1,0:T(8,128)}), f32[64,2,8,384]{3,2,1,0:T(8,128)S(1)}, u32[]{:S(2)}, u32[]{:S(2)}) async-start(f32[64,2,8,384]{3,2,1,0:T(8,128)} %copy.29), calls=%async_computation.1 | async-start | bytes 3145728 | tf_op jit(solution)/shard_map/all_to_all | solution.py:171
  146.0 0.6 gather_fusion
  146.6 0.8 bitcast_select_fusion
  147.3 19.3 %all-to-all-done.1 = f32[64,2,8,384]{3,2,1,0:T(8,128)S(1)} async-done(((f32[64,2,8,384]{3,2,1,0:T(8,128)}), f32[64,2,8,384]{3,2,1,0:T(8,128)S(1)}, u32[]{:S(2)}, u32[]{:S(2)}) %all-to-all-start.1) | async-done | bytes 1572896 | tf_op jit(solution)/shard_map/all_to_all | solution.py:171
  166.6 1.3 copy.40
  (26 shorter events, 1.5 us)
Async XLA Ops:
  0.6 2.0 %copy-start = (s32[32,5]{0,1:T(8,128)S(1)}, s32[32,5]{0,1:T(8,128)}, u32[]{:S(2)}) copy-start(s32[32,5]{0,1:T(8,128)} %param.11) | copy-start | bytes 1924
  0.6 20.2 %collective-permute-start = (f32[8,2,64,384]{3,2,1,0:T(8,128)}, f32[8,2,64,384]{3,2,1,0:T(8,128)S(1)}, u32[]{:S(2)}, u32[]{:S(2)}) collective-permute-start(f32[8,2,64,384]{3,2,1,0:T(8,128)} %top_ref.1), channel_id=1, source_target_pairs={{1,0},{2,1},{3,2},{4,3},{5,4},{6,5},{7,6},{8,7},{9,8},{10,9},{11,1... | collective-permute-start | bytes 4718600 | tf_op jit(solution)/shard_map/ppermute | solution.py:18
  20.8 1.1 copy-start.1
  52.8 22.0 %collective-permute-start.1 = (f32[8,2,64,384]{3,2,1,0:T(8,128)}, f32[8,2,64,384]{3,2,1,0:T(8,128)S(1)}, u32[]{:S(2)}, u32[]{:S(2)}) collective-permute-start(f32[8,2,64,384]{3,2,1,0:T(8,128)} %get-tuple-element.5), channel_id=1, source_target_pairs={{0,1},{1,2},{2,3},{3,4},{4,5},{5,6},{6,7},{7,8},{8,9},{9,10},{10,1... | collective-permute-start | bytes 4718600 | tf_op jit(solution)/shard_map/ppermute | solution.py:18
  78.7 9.7 %copy-start.2 = (f32[64,2,8]{0,2,1:T(8,128)S(1)}, f32[64,2,8]{0,2,1:T(8,128)}, u32[]{:S(2)}) copy-start(f32[64,2,8]{0,2,1:T(8,128)} %param.12) | copy-start | bytes 12292
  78.7 50.8 %all-to-all-start = ((f32[8,2,64,384]{3,1,0,2:T(2,128)}), f32[8,2,64,384]{3,1,0,2:T(2,128)S(1)}, u32[]{:S(2)}, u32[]{:S(2)}) async-start(f32[8,2,64,384]{3,1,0,2:T(2,128)} %copy.26), calls=%async_computation | async-start | bytes 3145728 | tf_op jit(solution)/shard_map/all_to_all | solution.py:166
  134.6 11.3 %copy-start.3 = (s32[8]{0:T(128)S(1)}, s32[8]{0:T(128)}, u32[]{:S(2)}) copy-start(s32[8]{0:T(128)} %param.13) | copy-start | bytes 100
  134.6 32.0 %all-to-all-start.1 = ((f32[64,2,8,384]{3,2,1,0:T(8,128)}), f32[64,2,8,384]{3,2,1,0:T(8,128)S(1)}, u32[]{:S(2)}, u32[]{:S(2)}) async-start(f32[64,2,8,384]{3,2,1,0:T(8,128)} %copy.29), calls=%async_computation.1 | async-start | bytes 3145728 | tf_op jit(solution)/shard_map/all_to_all | solution.py:171
